TPU v7x, 512 devices: a whole 4x8x8 slice. The times are simulated.
512 devices in a mesh: grp: 16 (over z, core), tile: 32 (over y, x).
Axes of the slice: x: 4, y: 8, z: 8, core: 2. Of those that a mesh axis runs over, the one named last changes fastest.
Arguments:
- tracer_adjoint: float32 [2, 96, 128, 4096], P(None, 'tile', 'grp'), may hold values from -6 to 6
- surface_adjoint: float32 [128, 4096], P('grp', 'tile'), may hold values from -6 to 6
- velocity: bfloat16 [2, 96, 128, 4096], P(None, 'tile', 'grp'), may hold values from -0.5 to 0.5
- vertical_coupling: float32 [96, 128, 4096], P(None, 'grp', 'tile'), may hold values from 0.05 to 3000, as said below
- ocean_levels: int32 [128, 4096], P('grp', 'tile'), may hold values from 0 to 96, as said below
- face_conductance: float32 [4, 128, 4096], P(None, 'grp', 'tile'), may hold values from 0.5 to 8, as said below
- buoyancy_weights: float32 [2, 96], replicated, may hold values from -1 to 1
- surface_flux: float32 [2], replicated, may hold values from 0.5 to 2
Outputs:
- tracer_result: float32 [2, 96, 128, 4096], P(None, 'tile', 'grp')
- surface_result: float32 [128, 4096], P('grp', 'tile')
Inputs may be any that keep to these rules, and one draw needn't show every extreme that they name: The faces agree between cells: face_conductance[1] of a cell equals face_conductance[0] of the cell to its west, and face_conductance[3] equals face_conductance[2] of the cell to its south, where such cells exist. `vertical_coupling`: mixing coefficients are positive. `ocean_levels`: wet levels of a column, from land to the full depth of 96 levels.
All inputs are finite; a program needn't handle non-finite values.
Results may differ from a plain program's by a relative error of at most 0.0003.
Values may be sent and summed in bfloat16 or wider, within the bound.
A program may use at most 64 MiB of HBM per device.

v0:
```python
import functools

import jax
import jax.numpy as jnp
from jax import lax
from jax.experimental import pallas as pl
from jax.experimental.pallas import tpu as pltpu
from jax.sharding import PartitionSpec as P

SOLVE_ITERS = 12
STEPS = 2
DIFFUSION = 0.1
MESH = pl.DeviceIdType.MESH
ROWS = 8
LANES = 128
UP, SIDE = 2, 1
HIGH, WIDE = (2 * UP + 1) * ROWS, (2 * SIDE + 1) * LANES


def wrap(value, size):
    return lax.rem(value + 2 * size, size)


def push(src, dst, send_sem, recv_sem, device):
    copy = pltpu.make_async_remote_copy(
        src_ref=src,
        dst_ref=dst,
        send_sem=send_sem,
        recv_sem=recv_sem,
        device_id=device,
        device_id_type=MESH,
    )
    return copy


def landed(ref, sem):
    pltpu.make_async_copy(ref, ref, sem).wait()


def kernel(
    sizes,
    tracer,
    surface,
    velocity,
    coupling,
    ocean_levels,
    conductance,
    weights,
    flux,
    tracer_out,
    surface_out,
    columns,
    currents,
    back,
    cond_region,
    surf_region,
    folded,
    inverse,
    lower,
    forward,
    grad,
    partial,
    surf_block,
    lane_send,
    lane_recv,
    row_send,
    row_recv,
    column_sems,
    current_sems,
    back_sems,
    cond_sems,
    surf_sems,
    lane_sems,
    row_sems,
):
    groups, tiles, share, levels = sizes
    group = lax.axis_index("grp")
    tile = lax.axis_index("tile")
    depth = ocean_levels[...]

    near = [
        (a, b)
        for a in range(2 * UP + 1)
        for b in range(2 * SIDE + 1)
        if (a, b) != (UP, SIDE)
    ]

    def near_device(a, b):
        return (wrap(group - (a - UP), groups), wrap(tile - (b - SIDE), tiles))

    barrier = pltpu.get_barrier_semaphore()

    def greet(i, _):
        pl.semaphore_signal(
            barrier, inc=1, device_id=(group, wrap(tile + i, tiles)), device_id_type=MESH
        )
        return 0

    lax.fori_loop(1, tiles, greet, 0)
    greeted = tiles - 1
    for a, b in near:
        if a != UP:
            greeted += 1
            pl.semaphore_signal(barrier, inc=1, device_id=near_device(a, b), device_id_type=MESH)
    pl.semaphore_wait(barrier, greeted)

    def block(a, b):
        return (pl.ds(a * ROWS, ROWS), pl.ds(b * LANES, LANES))

    def cond_copy(n):
        a, b = near[n]
        rows, lanes = block(a, b)
        return push(
            conductance,
            cond_region.at[:, rows, lanes],
            cond_sems.at[0, n],
            cond_sems.at[1, n],
            near_device(a, b),
        )

    def surf_copy(step, n):
        a, b = near[n]
        rows, lanes = block(a, b)
        return push(
            surface if step == 0 else surf_block,
            surf_region.at[step, rows, lanes],
            surf_sems.at[step, 0, n],
            surf_sems.at[step, 1, n],
            near_device(a, b),
        )

    for n in range(len(near)):
        cond_copy(n).start()
        surf_copy(0, n).start()

    def lanes_of(i):
        return pl.ds(pl.multiple_of(i * LANES, LANES), LANES)

    def column_copy(to):
        return push(
            tracer.at[:, :, :, lanes_of(to)],
            columns.at[:, pl.ds(tile * share, share)],
            column_sems.at[0, to],
            column_sems.at[1, tile],
            (group, to),
        )

    def current_copy(to):
        return push(
            velocity.at[:, :, :, lanes_of(to)],
            currents.at[:, pl.ds(tile * share, share)],
            current_sems.at[0, to],
            current_sems.at[1, tile],
            (group, to),
        )

    def back_copy(to):
        return push(
            partial.at[:, pl.ds(to * share, share)],
            back.at[:, :, :, lanes_of(tile)],
            back_sems.at[0, to],
            back_sems.at[1, tile],
            (group, to),
        )

    def others(action):
        def one(i, _):
            action(wrap(tile + i, tiles))
            return 0

        lax.fori_loop(1, tiles, one, 0)

    others(lambda to: column_copy(to).start())
    own_column = pltpu.make_async_copy(
        tracer.at[:, :, :, lanes_of(tile)],
        columns.at[:, pl.ds(tile * share, share)],
        column_sems.at[1, tile],
    )
    own_column.start()
    others(lambda to: current_copy(to).start())
    own_current = pltpu.make_async_copy(
        velocity.at[:, :, :, lanes_of(tile)],
        currents.at[:, pl.ds(tile * share, share)],
        current_sems.at[1, tile],
    )
    own_current.start()

    own_rows, own_lanes = block(UP, SIDE)
    cond_region[:, own_rows, own_lanes] = conductance[...]
    surf_region[0, own_rows, own_lanes] = surface[...]

    def factor(k, carry):
        previous, level_coup = carry
        following = jnp.where(k + 1 < depth, coupling[jnp.minimum(k + 1, levels - 1)], 0.0)
        diagonal = 1.0 + level_coup + following
        reciprocal = 1.0 / (diagonal - level_coup * previous)
        ahead = following * reciprocal
        inverse[k] = reciprocal
        lower[k] = level_coup * reciprocal
        forward[k] = ahead
        return (ahead, following)

    nothing = jnp.zeros((ROWS, LANES), jnp.float32)
    lax.fori_loop(0, levels, factor, (nothing, nothing))

    row_at = lax.broadcasted_iota(jnp.int32, (HIGH, WIDE), 0) + (group - UP) * ROWS
    lane_at = lax.broadcasted_iota(jnp.int32, (HIGH, WIDE), 1) + (tile - SIDE) * LANES
    inside = (
        (row_at >= 0)
        & (row_at < groups * ROWS)
        & (lane_at >= 0)
        & (lane_at < tiles * LANES)
    )

    for n in range(len(near)):
        rows, lanes = block(*near[n])
        landed(cond_region.at[:, rows, lanes], cond_sems.at[1, n])
    faces = [jnp.where(inside, cond_region[f], 0.0) for f in range(4)]
    region_recip = 1.0 / (1.0 + faces[0] + faces[1] + faces[2] + faces[3])
    for f in range(4):
        folded[f] = faces[f] * region_recip
    folded[4] = region_recip

    def relax(step):
        for n in range(len(near)):
            rows, lanes = block(*near[n])
            landed(surf_region.at[step, rows, lanes], surf_sems.at[step, 1, n])
        source = jnp.where(inside, surf_region[step], 0.0)
        scaled = source * folded[4]

        def sweep(_, iterate):
            return (
                scaled
                + folded[0] * pltpu.roll(iterate, WIDE - 1, 1)
                + folded[1] * pltpu.roll(iterate, 1, 1)
                + folded[2] * pltpu.roll(iterate, HIGH - 1, 0)
                + folded[3] * pltpu.roll(iterate, 1, 0)
            )

        solved = lax.fori_loop(0, SOLVE_ITERS, sweep, source)
        return solved[UP * ROWS : (UP + 1) * ROWS, SIDE * LANES : (SIDE + 1) * LANES]

    lane = lax.broadcasted_iota(jnp.int32, (ROWS, LANES), 1)
    row = lax.broadcasted_iota(jnp.int32, (ROWS, LANES), 0)

    def downward(k, sources, relaxed, carry):
        wet = jnp.where(k < depth, relaxed, 0.0)
        level_inv, level_low = inverse[k], lower[k]
        done = []
        for a in range(2):
            current = (sources[a] + weights[a, k] * wet) * level_inv + level_low * carry[a]
            grad[a, k] = current
            done.append(current)
        return tuple(done)

    def upward():
        def one(j, carry):
            for u in range(share):
                k = levels - 1 - (j * share + u)
                ahead = forward[k]
                wet = k < depth
                carry = tuple(grad[a, k] + ahead * carry[a] for a in range(2))
                for a in range(2):
                    grad[a, k] = jnp.where(wet, carry[a], 0.0)
            return carry

        return lax.fori_loop(0, tiles, one, (nothing, nothing))

    def next_surface(relaxed, top):
        return relaxed + jnp.where(0 < depth, flux[0] * top[0] + flux[1] * top[1], 0.0)

    def spread(step):
        def one(j, carry):
            carry = list(carry)
            for u in range(share):
                k = j * share + u
                zonal = 0.5 * currents[0, k].astype(jnp.float32)
                meridional = 0.5 * currents[1, k].astype(jnp.float32)
                to_west, to_east = DIFFUSION + zonal, DIFFUSION - zonal
                to_south, to_north = DIFFUSION + meridional, DIFFUSION - meridional
                for a in range(2):
                    masked = grad[a, k]
                    from_east = pltpu.roll(masked * to_west, LANES - 1, 1)
                    from_west = pltpu.roll(masked * to_east, 1, 1)
                    southward = masked * to_south
                    from_north = pltpu.roll(southward, ROWS - 1, 0)
                    from_south = pltpu.roll(masked * to_north, 1, 0)
                    partial[a, k] = (
                        (1.0 - 4.0 * DIFFUSION) * masked
                        + jnp.where(lane == LANES - 1, 0.0, from_east)
                        + jnp.where(lane == 0, 0.0, from_west)
                        + jnp.where(row == ROWS - 1, 0.0, from_north)
                        + jnp.where(row == 0, 0.0, from_south)
                    )
                    carry[2 * a] = jnp.where(
                        lane == k, pltpu.roll(from_east, k + 1, 1), carry[2 * a]
                    )
                    carry[2 * a + 1] = jnp.where(
                        lane == k, pltpu.roll(from_west, k, 1), carry[2 * a + 1]
                    )
                    row_send[step, 0, a, pl.ds(k, 1), :] = southward[0:1]
                    row_send[step, 1, a, pl.ds(k, 1), :] = from_south[0:1]
            return tuple(carry)

        edges = lax.fori_loop(0, tiles, one, (nothing,) * 4)
        for a in range(2):
            for side in range(2):
                lane_send[step, side, a] = edges[2 * a + side]

    def edge_copies(step):
        return [
            push(
                lane_send.at[step, side],
                lane_recv.at[step, side],
                lane_sems.at[step, 0, side],
                lane_sems.at[step, 1, side],
                (group, wrap(tile - 1 + 2 * side, tiles)),
            )
            for side in range(2)
        ] + [
            push(
                row_send.at[step, side],
                row_recv.at[step, side],
                row_sems.at[step, 0, side],
                row_sems.at[step, 1, side],
                (wrap(group - 1 + 2 * side, groups), tile),
            )
            for side in range(2)
        ]

    def edges_landed(step):
        for side in range(2):
            landed(lane_recv.at[step, side], lane_sems.at[step, 1, side])
            landed(row_recv.at[step, side], row_sems.at[step, 1, side])

    at_east = (lane == LANES - 1) & (tile < tiles - 1)
    at_west = (lane == 0) & (tile > 0)
    at_north = (row == ROWS - 1) & (group < groups - 1)
    at_south = (row == 0) & (group > 0)

    def gathered(step, a, k):
        east = pltpu.roll(lane_recv[step, 0, a], LANES - 1 - k, 1)
        west = pltpu.roll(lane_recv[step, 1, a], LANES - k, 1)
        north = jnp.broadcast_to(row_recv[step, 0, a, pl.ds(k, 1), :], (ROWS, LANES))
        south = jnp.broadcast_to(row_recv[step, 1, a, pl.ds(k, 1), :], (ROWS, LANES))
        return (
            partial[a, k]
            + jnp.where(at_east, east, 0.0)
            + jnp.where(at_west, west, 0.0)
            + jnp.where(at_north, north, 0.0)
            + jnp.where(at_south, south, 0.0)
        )

    relaxed = relax(0)

    def first_down(s, carry):
        landed(columns.at[:, pl.ds(s * share, share)], column_sems.at[1, s])
        for u in range(share):
            k = s * share + u
            carry = downward(k, [columns[0, k], columns[1, k]], relaxed, carry)
        return carry

    lax.fori_loop(0, tiles, first_down, (nothing, nothing))
    top = upward()
    surf_block[...] = next_surface(relaxed, top)
    surf_region[1, own_rows, own_lanes] = surf_block[...]
    for n in range(len(near)):
        surf_copy(1, n).start()

    def current_landed(s, _):
        landed(currents.at[:, pl.ds(s * share, share)], current_sems.at[1, s])
        return 0

    lax.fori_loop(0, tiles, current_landed, 0)
    spread(0)
    for copy in edge_copies(0):
        copy.start()

    relaxed_again = relax(1)
    edges_landed(0)

    def second_down(s, carry):
        for u in range(share):
            k = s * share + u
            carry = downward(k, [gathered(0, a, k) for a in range(2)], relaxed_again, carry)
        return carry

    lax.fori_loop(0, tiles, second_down, (nothing, nothing))
    top = upward()
    surface_out[...] = next_surface(relaxed_again, top)
    spread(1)
    for copy in edge_copies(1):
        copy.start()
    edges_landed(1)

    def finish(i, _):
        to = wrap(tile + i, tiles)
        for u in range(share):
            k = to * share + u
            for a in range(2):
                partial[a, k] = gathered(1, a, k)
        return 0

    lax.fori_loop(0, tiles, finish, 0)
    others(lambda to: back_copy(to).start())
    own_back = pltpu.make_async_copy(
        partial.at[:, pl.ds(tile * share, share)],
        back.at[:, :, :, lanes_of(tile)],
        back_sems.at[1, tile],
    )
    own_back.start()

    def back_landed(s, _):
        landed(back.at[:, :, :, lanes_of(s)], back_sems.at[1, s])
        return 0

    lax.fori_loop(0, tiles, back_landed, 0)
    tracer_out[...] = back[...]

    others(lambda to: column_copy(to).wait_send())
    others(lambda to: current_copy(to).wait_send())
    others(lambda to: back_copy(to).wait_send())
    for n in range(len(near)):
        cond_copy(n).wait_send()
        for step in range(STEPS):
            surf_copy(step, n).wait_send()
    for step in range(STEPS):
        for copy in edge_copies(step):
            copy.wait_send()


def local(
    tracer_adjoint,
    surface_adjoint,
    velocity,
    vertical_coupling,
    ocean_levels,
    face_conductance,
    buoyancy_weights,
    surface_flux,
):
    groups, tiles = lax.axis_size("grp"), lax.axis_size("tile")
    levels = vertical_coupling.shape[0]
    share = levels // tiles
    cells = (ROWS, LANES)
    near = (2 * UP + 1) * (2 * SIDE + 1) - 1
    f32 = jnp.float32
    vmem = pl.BlockSpec(memory_space=pltpu.VMEM)
    smem = pl.BlockSpec(memory_space=pltpu.SMEM)
    dma = pltpu.SemaphoreType.DMA
    return pl.pallas_call(
        functools.partial(kernel, (groups, tiles, share, levels)),
        out_shape=(
            jax.ShapeDtypeStruct(tracer_adjoint.shape, f32),
            jax.ShapeDtypeStruct(surface_adjoint.shape, f32),
        ),
        in_specs=[vmem] * 6 + [smem] * 2,
        out_specs=(vmem, vmem),
        scratch_shapes=[
            pltpu.VMEM((2, levels) + cells, f32),
            pltpu.VMEM((2, levels) + cells, jnp.bfloat16),
            pltpu.VMEM(tracer_adjoint.shape, f32),
            pltpu.VMEM((4, HIGH, WIDE), f32),
            pltpu.VMEM((STEPS, HIGH, WIDE), f32),
            pltpu.VMEM((5, HIGH, WIDE), f32),
            pltpu.VMEM((levels,) + cells, f32),
            pltpu.VMEM((levels,) + cells, f32),
            pltpu.VMEM((levels,) + cells, f32),
            pltpu.VMEM((2, levels) + cells, f32),
            pltpu.VMEM((2, levels) + cells, f32),
            pltpu.VMEM(cells, f32),
            pltpu.VMEM((STEPS, 2, 2) + cells, f32),
            pltpu.VMEM((STEPS, 2, 2) + cells, f32),
            pltpu.VMEM((STEPS, 2, 2, levels, LANES), f32),
            pltpu.VMEM((STEPS, 2, 2, levels, LANES), f32),
            dma((2, tiles)),
            dma((2, tiles)),
            dma((2, tiles)),
            dma((2, near)),
            dma((STEPS, 2, near)),
            dma((STEPS, 2, 2)),
            dma((STEPS, 2, 2)),
        ],
        compiler_params=pltpu.CompilerParams(collective_id=0, has_side_effects=True),
    )(
        tracer_adjoint,
        surface_adjoint,
        velocity,
        vertical_coupling,
        ocean_levels,
        face_conductance,
        buoyancy_weights,
        surface_flux,
    )


def solution(mesh):
    in_specs = (
        P(None, "tile", "grp", None),
        P("grp", "tile"),
        P(None, "tile", "grp", None),
        P(None, "grp", "tile"),
        P("grp", "tile"),
        P(None, "grp", "tile"),
        P(),
        P(),
    )
    out_specs = (P(None, "tile", "grp", None), P("grp", "tile"))
    return jax.shard_map(local, mesh=mesh, in_specs=in_specs, out_specs=out_specs, check_vma=False)
```

profile of v0, /device:TPU:6, one launch (start us, length us, event | category | flops | bytes accessed | tf_op | source)
XLA Modules:
  0.0 98.0 jit_solution(17972745165842947327)
XLA Ops:
  0.6 94.7 %shard_map.95 = (f32[2,3,8,4096]{3,2,1,0:T(8,128)}, f32[8,128]{1,0:T(8,128)}) custom-call(f32[2,3,8,4096]{3,2,1,0:T(8,128)} %tracer.1, f32[8,128]{1,0:T(8,128)} %surface.1, bf16[2,3,8,4096]{3,2,1,0:T(8,128)(2,1)} %velocity.1, f32[96,8,128]{2,1,0:T(8,128)} %coupling.1, s32[8,128]{1,0:T(8,128)} %ocean_levels.1, f32[4,8,128]{2,1,0:T(8,128)} %conductance.1, ...), custom_call_target="tpu_custom_call" | custom-call | tf_op jit(solution)/shard_map/pallas_call | solution.py:451
  95.3 0.0 copy-start
  95.3 2.1 %copy.12 = f32[2,3,8,4096]{3,2,1,0:T(8,128)} copy(f32[2,3,8,4096]{3,2,1,0:T(8,128)} %get-tuple-element.4) | data formatting | bytes 1572864
  97.4 0.0 copy-done
  97.4 0.6 copy.13
Async XLA Ops:
  95.3 2.1 %copy-start = (f32[8,128]{1,0:T(8,128)S(1)}, f32[8,128]{1,0:T(8,128)}, u32[]{:S(2)}) copy-start(f32[8,128]{1,0:T(8,128)} %get-tuple-element.5) | copy-start | bytes 12292
where the time goes:
time: 98.1 us; the launch traced here: 98 us
  Pallas kernels  94.7 us (97%)
  local copies, waits for them, and re-layouts  2.66 us (3%)
    pallas_call x1, Pallas kernels, local(): pl.pallas_call(functools.partial(kernel, (groups, tiles, share, levels)),...  94.7 us
    unnamed x4, local copies, waits for them, and re-layouts  2.66 us

commit v1 on v0

--- a/solution.py
+++ b/solution.py
@@ -10,6 +10,7 @@
 SOLVE_ITERS = 12
 STEPS = 2
 DIFFUSION = 0.1
+CODE_MAX = 32767.0
 MESH = pl.DeviceIdType.MESH
 ROWS = 8
 LANES = 128
@@ -37,21 +38,45 @@
     pltpu.make_async_copy(ref, ref, sem).wait()
 
 
+def block(a, b):
+    return (pl.ds(a * ROWS, ROWS), pl.ds(b * LANES, LANES))
+
+
+def lanes_of(i):
+    return pl.ds(pl.multiple_of(i * LANES, LANES), LANES)
+
+
+def decode(word):
+    first = lax.shift_right_arithmetic(word + 32768, 16)
+    second = word - lax.shift_left(first, 16)
+    return (first.astype(jnp.float32), second.astype(jnp.float32))
+
+
 def kernel(
     sizes,
-    tracer,
+    tracer_in,
     surface,
     velocity,
-    coupling,
+    coupling_in,
     ocean_levels,
     conductance,
+    weights_in,
+    flux_in,
+    codes_out,
+    scales_out,
+    surface_out,
+    tracer,
+    coupling,
+    depths,
     weights,
     flux,
-    tracer_out,
-    surface_out,
-    columns,
+    sent_codes,
+    sent_scales,
+    codes,
+    scales,
     currents,
-    back,
+    back_codes,
+    back_scales,
     cond_region,
     surf_region,
     folded,
@@ -65,9 +90,12 @@
     lane_recv,
     row_send,
     row_recv,
-    column_sems,
+    local_sems,
+    code_sems,
+    scale_sems,
     current_sems,
-    back_sems,
+    back_code_sems,
+    back_scale_sems,
     cond_sems,
     surf_sems,
     lane_sems,
@@ -76,7 +104,23 @@
     groups, tiles, share, levels = sizes
     group = lax.axis_index("grp")
     tile = lax.axis_index("tile")
-    depth = ocean_levels[...]
+
+    own_rows, own_lanes = block(UP, SIDE)
+    loads = [
+        pltpu.make_async_copy(src, dst, local_sems.at[n])
+        for n, (src, dst) in enumerate(
+            [
+                (tracer_in, tracer),
+                (ocean_levels, depths),
+                (coupling_in, coupling),
+                (weights_in, weights),
+                (flux_in, flux),
+                (conductance, cond_region.at[:, own_rows, own_lanes]),
+                (surface, surf_region.at[0, own_rows, own_lanes]),
+            ]
+        )
+    ]
+    loads[0].start()
 
     near = [
         (a, b)
@@ -102,10 +146,29 @@
         if a != UP:
             greeted += 1
             pl.semaphore_signal(barrier, inc=1, device_id=near_device(a, b), device_id_type=MESH)
+    for load in loads[1:]:
+        load.start()
+
+    def encode(values, slot, code_ref, scale_ref):
+        rounded = []
+        for a in range(2):
+            peak = functools.reduce(jnp.maximum, [jnp.abs(v) for v in values[a]])
+            peak = jnp.maximum(jnp.max(peak, axis=0, keepdims=True), 1e-30)
+            gain = jnp.broadcast_to(CODE_MAX / peak, (ROWS, LANES))
+            scale_ref[slot, pl.ds(a, 1), :] = peak * (1.0 / CODE_MAX)
+            rounded.append([jnp.floor(v * gain + 0.5).astype(jnp.int32) for v in values[a]])
+        for u in range(share):
+            code_ref[slot, u] = lax.shift_left(rounded[0][u], 16) + rounded[1][u]
+
+    loads[0].wait()
+
+    def encode_tracer(to, _):
+        values = [[tracer[a, u, :, lanes_of(to)] for u in range(share)] for a in range(2)]
+        encode(values, to, sent_codes, sent_scales)
+        return 0
+
+    lax.fori_loop(0, tiles, encode_tracer, 0)
     pl.semaphore_wait(barrier, greeted)
-
-    def block(a, b):
-        return (pl.ds(a * ROWS, ROWS), pl.ds(b * LANES, LANES))
 
     def cond_copy(n):
         a, b = near[n]
@@ -133,16 +196,22 @@
         cond_copy(n).start()
         surf_copy(0, n).start()
 
-    def lanes_of(i):
-        return pl.ds(pl.multiple_of(i * LANES, LANES), LANES)
-
-    def column_copy(to):
-        return push(
-            tracer.at[:, :, :, lanes_of(to)],
-            columns.at[:, pl.ds(tile * share, share)],
-            column_sems.at[0, to],
-            column_sems.at[1, tile],
-            (group, to),
+    def code_copies(to):
+        return (
+            push(
+                sent_codes.at[to],
+                codes.at[tile],
+                code_sems.at[0, to],
+                code_sems.at[1, tile],
+                (group, to),
+            ),
+            push(
+                sent_scales.at[to],
+                scales.at[tile],
+                scale_sems.at[0, to],
+                scale_sems.at[1, tile],
+                (group, to),
+            ),
         )
 
     def current_copy(to):
@@ -154,14 +223,31 @@
             (group, to),
         )
 
-    def back_copy(to):
-        return push(
-            partial.at[:, pl.ds(to * share, share)],
-            back.at[:, :, :, lanes_of(tile)],
-            back_sems.at[0, to],
-            back_sems.at[1, tile],
-            (group, to),
-        )
+    def back_copies(to):
+        return (
+            push(
+                back_codes.at[to],
+                codes_out.at[:, :, lanes_of(tile)],
+                back_code_sems.at[0, to],
+                back_code_sems.at[1, tile],
+                (group, to),
+            ),
+            push(
+                back_scales.at[to],
+                scales_out.at[:, lanes_of(tile)],
+                back_scale_sems.at[0, to],
+                back_scale_sems.at[1, tile],
+                (group, to),
+            ),
+        )
+
+    def start(copies):
+        for copy in copies:
+            copy.start()
+
+    def sent(copies):
+        for copy in copies:
+            copy.wait_send()
 
     def others(action):
         def one(i, _):
@@ -170,13 +256,13 @@
 
         lax.fori_loop(1, tiles, one, 0)
 
-    others(lambda to: column_copy(to).start())
-    own_column = pltpu.make_async_copy(
-        tracer.at[:, :, :, lanes_of(tile)],
-        columns.at[:, pl.ds(tile * share, share)],
-        column_sems.at[1, tile],
+    others(lambda to: start(code_copies(to)))
+    start(
+        [
+            pltpu.make_async_copy(sent_codes.at[tile], codes.at[tile], code_sems.at[1, tile]),
+            pltpu.make_async_copy(sent_scales.at[tile], scales.at[tile], scale_sems.at[1, tile]),
+        ]
     )
-    own_column.start()
     others(lambda to: current_copy(to).start())
     own_current = pltpu.make_async_copy(
         velocity.at[:, :, :, lanes_of(tile)],
@@ -185,9 +271,9 @@
     )
     own_current.start()
 
-    own_rows, own_lanes = block(UP, SIDE)
-    cond_region[:, own_rows, own_lanes] = conductance[...]
-    surf_region[0, own_rows, own_lanes] = surface[...]
+    for load in loads[1:]:
+        load.wait()
+    depth = depths[...]
 
     def factor(k, carry):
         previous, level_coup = carry
@@ -270,8 +356,11 @@
         return relaxed + jnp.where(0 < depth, flux[0] * top[0] + flux[1] * top[1], 0.0)
 
     def spread(step):
-        def one(j, carry):
+        def one(i, carry):
             carry = list(carry)
+            j = wrap(tile - i, tiles)
+            if step == 0:
+                landed(currents.at[:, pl.ds(j * share, share)], current_sems.at[1, j])
             for u in range(share):
                 k = j * share + u
                 zonal = 0.5 * currents[0, k].astype(jnp.float32)
@@ -354,10 +443,13 @@
     relaxed = relax(0)
 
     def first_down(s, carry):
-        landed(columns.at[:, pl.ds(s * share, share)], column_sems.at[1, s])
+        landed(codes.at[s], code_sems.at[1, s])
+        landed(scales.at[s], scale_sems.at[1, s])
+        factors = [scales[s, pl.ds(a, 1), :] for a in range(2)]
         for u in range(share):
             k = s * share + u
-            carry = downward(k, [columns[0, k], columns[1, k]], relaxed, carry)
+            values = decode(codes[s, u])
+            carry = downward(k, [values[a] * factors[a] for a in range(2)], relaxed, carry)
         return carry
 
     lax.fori_loop(0, tiles, first_down, (nothing, nothing))
@@ -367,11 +459,6 @@
     for n in range(len(near)):
         surf_copy(1, n).start()
 
-    def current_landed(s, _):
-        landed(currents.at[:, pl.ds(s * share, share)], current_sems.at[1, s])
-        return 0
-
-    lax.fori_loop(0, tiles, current_landed, 0)
     spread(0)
     for copy in edge_copies(0):
         copy.start()
@@ -393,33 +480,40 @@
         copy.start()
     edges_landed(1)
 
-    def finish(i, _):
-        to = wrap(tile + i, tiles)
-        for u in range(share):
-            k = to * share + u
-            for a in range(2):
-                partial[a, k] = gathered(1, a, k)
+    def finish(to):
+        values = [[gathered(1, a, to * share + u) for u in range(share)] for a in range(2)]
+        encode(values, to, back_codes, back_scales)
+
+    def finish_and_send(i, _):
+        finish(wrap(tile + i, tiles))
+        start(back_copies(wrap(tile + i - 1, tiles)))
         return 0
 
-    lax.fori_loop(0, tiles, finish, 0)
-    others(lambda to: back_copy(to).start())
-    own_back = pltpu.make_async_copy(
-        partial.at[:, pl.ds(tile * share, share)],
-        back.at[:, :, :, lanes_of(tile)],
-        back_sems.at[1, tile],
+    finish(wrap(tile + 1, tiles))
+    lax.fori_loop(2, tiles, finish_and_send, 0)
+    finish(tile)
+    start(back_copies(wrap(tile - 1, tiles)))
+    start(
+        [
+            pltpu.make_async_copy(
+                back_codes.at[tile], codes_out.at[:, :, lanes_of(tile)], back_code_sems.at[1, tile]
+            ),
+            pltpu.make_async_copy(
+                back_scales.at[tile], scales_out.at[:, lanes_of(tile)], back_scale_sems.at[1, tile]
+            ),
+        ]
     )
-    own_back.start()
 
     def back_landed(s, _):
-        landed(back.at[:, :, :, lanes_of(s)], back_sems.at[1, s])
+        landed(codes_out.at[:, :, lanes_of(s)], back_code_sems.at[1, s])
+        landed(scales_out.at[:, lanes_of(s)], back_scale_sems.at[1, s])
         return 0
 
     lax.fori_loop(0, tiles, back_landed, 0)
-    tracer_out[...] = back[...]
-
-    others(lambda to: column_copy(to).wait_send())
+
+    others(lambda to: sent(code_copies(to)))
     others(lambda to: current_copy(to).wait_send())
-    others(lambda to: back_copy(to).wait_send())
+    others(lambda to: sent(back_copies(to)))
     for n in range(len(near)):
         cond_copy(n).wait_send()
         for step in range(STEPS):
@@ -427,6 +521,14 @@
     for step in range(STEPS):
         for copy in edge_copies(step):
             copy.wait_send()
+
+
+def unpack(codes, scales, surface, tracer_out, surface_out):
+    for u in range(codes.shape[0]):
+        values = decode(codes[u])
+        for a in range(2):
+            tracer_out[a, u] = values[a] * scales[pl.ds(a, 1), :]
+    surface_out[...] = surface[...]
 
 
 def local(
@@ -444,22 +546,33 @@
     share = levels // tiles
     cells = (ROWS, LANES)
     near = (2 * UP + 1) * (2 * SIDE + 1) - 1
-    f32 = jnp.float32
+    f32, i32 = jnp.float32, jnp.int32
+    anywhere = pl.BlockSpec(memory_space=pl.ANY)
     vmem = pl.BlockSpec(memory_space=pltpu.VMEM)
-    smem = pl.BlockSpec(memory_space=pltpu.SMEM)
     dma = pltpu.SemaphoreType.DMA
-    return pl.pallas_call(
+    packed = (tiles, share) + cells
+    codes, scales, surface = pl.pallas_call(
         functools.partial(kernel, (groups, tiles, share, levels)),
         out_shape=(
-            jax.ShapeDtypeStruct(tracer_adjoint.shape, f32),
+            jax.ShapeDtypeStruct((share, ROWS, tiles * LANES), i32),
+            jax.ShapeDtypeStruct((2, tiles * LANES), f32),
             jax.ShapeDtypeStruct(surface_adjoint.shape, f32),
         ),
-        in_specs=[vmem] * 6 + [smem] * 2,
-        out_specs=(vmem, vmem),
+        in_specs=[anywhere] * 8,
+        out_specs=(anywhere, anywhere, vmem),
         scratch_shapes=[
-            pltpu.VMEM((2, levels) + cells, f32),
+            pltpu.VMEM(tracer_adjoint.shape, f32),
+            pltpu.VMEM(vertical_coupling.shape, f32),
+            pltpu.VMEM(cells, i32),
+            pltpu.SMEM(buoyancy_weights.shape, f32),
+            pltpu.SMEM(surface_flux.shape, f32),
+            pltpu.VMEM(packed, i32),
+            pltpu.VMEM((tiles, 2, LANES), f32),
+            pltpu.VMEM(packed, i32),
+            pltpu.VMEM((tiles, 2, LANES), f32),
             pltpu.VMEM((2, levels) + cells, jnp.bfloat16),
-            pltpu.VMEM(tracer_adjoint.shape, f32),
+            pltpu.VMEM(packed, i32),
+            pltpu.VMEM((tiles, 2, LANES), f32),
             pltpu.VMEM((4, HIGH, WIDE), f32),
             pltpu.VMEM((STEPS, HIGH, WIDE), f32),
             pltpu.VMEM((5, HIGH, WIDE), f32),
@@ -473,6 +586,9 @@
             pltpu.VMEM((STEPS, 2, 2) + cells, f32),
             pltpu.VMEM((STEPS, 2, 2, levels, LANES), f32),
             pltpu.VMEM((STEPS, 2, 2, levels, LANES), f32),
+            dma((7,)),
+            dma((2, tiles)),
+            dma((2, tiles)),
             dma((2, tiles)),
             dma((2, tiles)),
             dma((2, tiles)),
@@ -492,6 +608,15 @@
         buoyancy_weights,
         surface_flux,
     )
+    return pl.pallas_call(
+        unpack,
+        out_shape=(
+            jax.ShapeDtypeStruct(tracer_adjoint.shape, f32),
+            jax.ShapeDtypeStruct(surface_adjoint.shape, f32),
+        ),
+        in_specs=[vmem] * 3,
+        out_specs=(vmem, vmem),
+    )(codes, scales, surface)
 
 
 def solution(mesh):

time: 98.1 us -> 77.6 us (0.79)
  the two profiles are of different devices: /device:TPU:6 before, /device:TPU:1 now
where the time goes in v1:
time: 77.6 us; the launch traced here: 77.4 us
  Pallas kernels  76.8 us (99%)
    pallas_call x1, Pallas kernels, local(): pl.pallas_call(functools.partial(kernel, (groups, tiles, share, levels)),...  74.8 us
    pallas_call x1, Pallas kernels, local(): pl.pallas_call(unpack, out_shape=(jax.ShapeDtypeStruct(tracer_adjoint.sha...  2.01 us

profile of v1, /device:TPU:1, one launch (start us, length us, event | category | flops | bytes accessed | tf_op | source)
XLA Modules:
  0.0 77.4 jit_solution(10177294940765384324)
XLA Ops:
  0.6 74.8 %shard_map.95 = (s32[3,8,4096]{2,1,0:T(8,128)}, f32[2,4096]{1,0:T(2,128)}, f32[8,128]{1,0:T(8,128)}) custom-call(f32[2,3,8,4096]{3,2,1,0:T(8,128)} %tracer_in.1, f32[8,128]{1,0:T(8,128)} %surface.1, bf16[2,3,8,4096]{3,2,1,0:T(8,128)(2,1)} %velocity.1, f32[96,8,128]{2,1,0:T(8,128)} %coupling_in.1, s32[8,128]{1,0:T(8,128)} %ocean_levels.1, ...), custom_call_target="tpu_custom_call" | custom-call | tf_op jit(solution)/shard_map/pallas_call | solution.py:554
  75.4 2.0 %shard_map.96 = (f32[2,3,8,4096]{3,2,1,0:T(8,128)}, f32[8,128]{1,0:T(8,128)}) custom-call(s32[3,8,4096]{2,1,0:T(8,128)} %get-tuple-element.5.codes, f32[2,4096]{1,0:T(2,128)} %get-tuple-element.6.scales, f32[8,128]{1,0:T(8,128)} %get-tuple-element.7.surface), custom_call_target="tpu_custom_call" | custom-call | tf_op jit(solution)/shard_map/pallas_call | solution.py:611

commit v2 on v1

v2 whole, which is shorter than its diff:
```python
import functools

import jax
import jax.numpy as jnp
from jax import lax
from jax.experimental import pallas as pl
from jax.experimental.pallas import tpu as pltpu
from jax.sharding import PartitionSpec as P

SOLVE_ITERS = 12
STEPS = 2
DIFFUSION = 0.1
CODE_MAX = 32767.0
MESH = pl.DeviceIdType.MESH
ROWS = 8
LANES = 128
UP = 2
HIGH = (2 * UP + 1) * ROWS
EDGE = 16
FIELDS = 4
QUAD = 4
CHUNKS = 2
EARLY = 8


def wrap(value, size):
    return lax.rem(value + 2 * size, size)


def push(src, dst, send_sem, recv_sem, device):
    return pltpu.make_async_remote_copy(
        src_ref=src,
        dst_ref=dst,
        send_sem=send_sem,
        recv_sem=recv_sem,
        device_id=device,
        device_id_type=MESH,
    )


def landed(ref, sem):
    pltpu.make_async_copy(ref, ref, sem).wait()


def lanes_of(i):
    return pl.ds(pl.multiple_of(i * LANES, LANES), LANES)


def decode(word):
    first = lax.shift_right_arithmetic(word + 32768, 16)
    second = word - lax.shift_left(first, 16)
    return (first.astype(jnp.float32), second.astype(jnp.float32))


def kernel(
    sizes,
    tracer_in,
    surface_in,
    velocity,
    coupling_in,
    ocean_levels,
    conductance_in,
    weights_in,
    flux_in,
    codes_out,
    scales_out,
    surface_out,
    tracer,
    surface,
    coupling,
    depths,
    conductance,
    weights,
    flux,
    sent_codes,
    sent_scales,
    codes,
    scales,
    currents,
    back_codes,
    back_scales,
    mine,
    mine_edge,
    middle,
    sides,
    around,
    fields,
    folded,
    inverse,
    lower,
    forward,
    grad,
    partial,
    surf_block,
    lane_send,
    lane_recv,
    row_send,
    row_recv,
    load_sems,
    code_sems,
    scale_sems,
    current_sems,
    send_sems,
    back_sems,
    near_sems,
    lane_sems,
    row_sems,
):
    groups, tiles, share, levels = sizes
    quads = tiles // QUAD
    deep = QUAD * share
    group = lax.axis_index("grp")
    tile = lax.axis_index("tile")
    near = [
        (a, b) for a in range(2 * UP + 1) for b in range(3) if (a, b) != (UP, 1)
    ]

    def near_device(a, b):
        return (wrap(group - (a - UP), groups), wrap(tile - (b - 1), tiles))

    loads = [
        pltpu.make_async_copy(src, dst, load_sems.at[n])
        for n, (src, dst) in enumerate(
            [
                (tracer_in, tracer),
                (conductance_in, conductance),
                (surface_in, surface),
                (ocean_levels, depths),
                (coupling_in, coupling),
                (weights_in, weights),
                (flux_in, flux),
            ]
        )
    ]
    loads[0].start()

    barrier = pltpu.get_barrier_semaphore()

    def greet(i, _):
        pl.semaphore_signal(
            barrier, inc=1, device_id=(group, wrap(tile + i, tiles)), device_id_type=MESH
        )
        return 0

    lax.fori_loop(1, tiles, greet, 0)
    greeted = tiles - 1
    for a, b in near:
        if a != UP:
            greeted += 1
            pl.semaphore_signal(barrier, inc=1, device_id=near_device(a, b), device_id_type=MESH)
    for load in loads[1:]:
        load.start()
    pl.semaphore_wait(barrier, greeted)

    def others(action, first=1, last=tiles):
        def one(i, _):
            action(wrap(tile + i, tiles))
            return 0

        lax.fori_loop(first, last, one, 0)

    def send_current(to):
        push(
            velocity.at[:, :, :, lanes_of(to)],
            currents.at[:, pl.ds(tile * share, share)],
            send_sems.at[0],
            current_sems.at[tile],
            (group, to),
        ).start()

    others(send_current, 1, 1 + EARLY)
    pltpu.make_async_copy(
        velocity.at[:, :, :, lanes_of(tile)],
        currents.at[:, pl.ds(tile * share, share)],
        current_sems.at[tile],
    ).start()

    lane = lax.broadcasted_iota(jnp.int32, (ROWS, LANES), 1)
    row = lax.broadcasted_iota(jnp.int32, (ROWS, LANES), 0)
    loads[1].wait()
    loads[2].wait()
    own = [
        conductance[0],
        conductance[2],
        1.0 / (1.0 + conductance[0] + conductance[1] + conductance[2] + conductance[3]),
        surface[...],
    ]
    packed = own[0]
    for f in range(FIELDS):
        mine[f] = own[f]
        western = own[f] if f == 0 else pltpu.roll(own[f], EDGE * f, 1)
        eastern = pltpu.roll(own[f], LANES // 2 + EDGE * (f + 1), 1)
        packed = jnp.where((lane >= EDGE * f) & (lane < EDGE * (f + 1)), western, packed)
        packed = jnp.where(
            (lane >= LANES // 2 + EDGE * f) & (lane < LANES // 2 + EDGE * (f + 1)), eastern, packed
        )
    mine_edge[...] = packed

    def encode(values, slot, code_ref, scale_ref):
        rounded = []
        for a in range(2):
            peak = functools.reduce(jnp.maximum, [jnp.abs(v) for v in values[a]])
            peak = jnp.maximum(jnp.max(peak, axis=0, keepdims=True), 1e-30)
            gain = jnp.broadcast_to(CODE_MAX / peak, (ROWS, LANES))
            scale_ref[slot, pl.ds(a, 1), :] = peak * (1.0 / CODE_MAX)
            rounded.append([jnp.floor(v * gain + 0.5).astype(jnp.int32) for v in values[a]])
        for u in range(share):
            code_ref[slot, u] = lax.shift_left(rounded[0][u], 16) + rounded[1][u]

    loads[0].wait()

    def encode_tracer(to, _):
        values = [[tracer[a, u, :, lanes_of(to)] for u in range(share)] for a in range(2)]
        encode(values, to, sent_codes, sent_scales)
        return 0

    lax.fori_loop(0, tiles, encode_tracer, 0)

    def middle_slot(a):
        return a if a < UP else a - 1

    for a, b in near:
        if b == 1:
            push(
                mine,
                middle.at[middle_slot(a)],
                send_sems.at[1],
                near_sems.at[0],
                near_device(a, b),
            ).start()
        else:
            push(
                mine_edge, sides.at[a, b // 2], send_sems.at[2], near_sems.at[1], near_device(a, b)
            ).start()

    def send_codes(to):
        push(
            sent_codes.at[to], codes.at[tile], send_sems.at[3], code_sems.at[tile], (group, to)
        ).start()
        push(
            sent_scales.at[to], scales.at[tile], send_sems.at[4], scale_sems.at[tile], (group, to)
        ).start()

    others(send_codes)
    pltpu.make_async_copy(sent_codes.at[tile], codes.at[tile], code_sems.at[tile]).start()
    pltpu.make_async_copy(sent_scales.at[tile], scales.at[tile], scale_sems.at[tile]).start()
    others(send_current, 1 + EARLY, tiles)
    for load in loads[3:]:
        load.wait()
    depth = depths[...]

    def factor(k, carry):
        previous, level_coup = carry
        following = jnp.where(k + 1 < depth, coupling[jnp.minimum(k + 1, levels - 1)], 0.0)
        diagonal = 1.0 + level_coup + following
        reciprocal = 1.0 / (diagonal - level_coup * previous)
        ahead = following * reciprocal
        inverse[k] = reciprocal
        lower[k] = level_coup * reciprocal
        forward[k] = ahead
        return (ahead, following)

    nothing = jnp.zeros((ROWS, LANES), jnp.float32)
    lax.fori_loop(0, levels, factor, (nothing, nothing))

    row_inside = [
        (group + (a - UP) >= 0) & (group + (a - UP) < groups) for a in range(2 * UP + 1)
    ]
    east_lanes = lane < EDGE
    side_inside = (east_lanes & (tile < tiles - 1)) | ((lane >= LANES - EDGE) & (tile > 0))

    def place(f, a, middle_block, side_block):
        rows = pl.ds(a * ROWS, ROWS)
        fields[f, rows, pl.ds(0, LANES)] = jnp.where(row_inside[a], middle_block, 0.0)
        fields[f, rows, pl.ds(LANES, LANES)] = jnp.where(
            side_inside & row_inside[a], side_block, 0.0
        )

    landed(middle, near_sems.at[0])
    landed(sides, near_sems.at[1])
    for a in range(2 * UP + 1):
        from_west, from_east = sides[a, 0], sides[a, 1]
        for f in range(FIELDS):
            east = from_east if f == 0 else pltpu.roll(from_east, LANES - EDGE * f, 1)
            west = pltpu.roll(from_west, (LANES // 2 - EDGE * (f + 1)) % LANES, 1)
            place(
                f,
                a,
                mine[f] if a == UP else middle[middle_slot(a), f],
                jnp.where(east_lanes, east, west),
            )
    eastern, northern, region_recip = fields[0], fields[1], fields[2]
    folded[0] = eastern * region_recip
    folded[1] = pltpu.roll(eastern, 1, 1) * region_recip
    folded[2] = northern * region_recip
    folded[3] = pltpu.roll(northern, 1, 0) * region_recip

    def relax():
        source = fields[FIELDS - 1]
        scaled = source * fields[2]

        def sweep(_, iterate):
            return (
                scaled
                + folded[0] * pltpu.roll(iterate, 2 * LANES - 1, 1)
                + folded[1] * pltpu.roll(iterate, 1, 1)
                + folded[2] * pltpu.roll(iterate, HIGH - 1, 0)
                + folded[3] * pltpu.roll(iterate, 1, 0)
            )

        solved = lax.fori_loop(0, SOLVE_ITERS, sweep, source)
        return solved[UP * ROWS : (UP + 1) * ROWS, :LANES]

    def downward(k, sources, relaxed, carry):
        wet = jnp.where(k < depth, relaxed, 0.0)
        level_inv, level_low = inverse[k], lower[k]
        done = []
        for a in range(2):
            current = (sources[a] + weights[a, k] * wet) * level_inv + level_low * carry[a]
            grad[a, k] = current
            done.append(current)
        return tuple(done)

    def upward():
        def rise(j, carry):
            for u in range(deep):
                k = levels - 1 - (j * deep + u)
                ahead = forward[k]
                wet = k < depth
                carry = tuple(grad[a, k] + ahead * carry[a] for a in range(2))
                for a in range(2):
                    grad[a, k] = jnp.where(wet, carry[a], 0.0)
            return carry

        return lax.fori_loop(0, quads, rise, (nothing, nothing))

    def next_surface(relaxed, top):
        return relaxed + jnp.where(0 < depth, flux[0] * top[0] + flux[1] * top[1], 0.0)

    def row_place(quad, u):
        return (lax.rem(quad, CHUNKS), lax.div(quad, CHUNKS) * deep + u)

    def give(step, quad, carry):
        carry = list(carry)
        for u in range(deep):
            k = quad * deep + u
            chunk, place_at = row_place(quad, u)
            zonal = 0.5 * currents[0, k].astype(jnp.float32)
            meridional = 0.5 * currents[1, k].astype(jnp.float32)
            for a in range(2):
                masked = grad[a, k]
                westward = masked * (DIFFUSION + zonal)
                eastward = masked * (DIFFUSION - zonal)
                southward = masked * (DIFFUSION + meridional)
                northward = pltpu.roll(masked * (DIFFUSION - meridional), 1, 0)
                partial[a, k] = (
                    (1.0 - 4.0 * DIFFUSION) * masked
                    + jnp.where(lane == LANES - 1, 0.0, pltpu.roll(westward, LANES - 1, 1))
                    + jnp.where(lane == 0, 0.0, pltpu.roll(eastward, 1, 1))
                    + jnp.where(row == ROWS - 1, 0.0, pltpu.roll(southward, ROWS - 1, 0))
                    + jnp.where(row == 0, 0.0, northward)
                )
                at_level = lane == k
                carry[2 * a] = jnp.where(at_level, pltpu.roll(westward, k, 1), carry[2 * a])
                carry[2 * a + 1] = jnp.where(
                    at_level, pltpu.roll(eastward, k + 1, 1), carry[2 * a + 1]
                )
                row_send[step, 0, chunk, a, pl.ds(place_at, 1), :] = southward[0:1]
                row_send[step, 1, chunk, a, pl.ds(place_at, 1), :] = northward[0:1]
        return tuple(carry)

    def keep_edges(message, edges):
        for a in range(2):
            for side in range(2):
                lane_send[message, side, a] = edges[2 * a + side]

    def edge_copies(step, chunk=None):
        message = 0 if chunk is None else 1 + chunk
        copies = []
        for side in range(2):
            rows = [ref.at[step, side] for ref in (row_send, row_recv)]
            if chunk is not None:
                rows = [ref.at[chunk] for ref in rows]
            copies += [
                push(
                    lane_send.at[message, side],
                    lane_recv.at[message, side],
                    lane_sems.at[message, 0, side],
                    lane_sems.at[message, 1, side],
                    (group, wrap(tile - 1 + 2 * side, tiles)),
                ),
                push(
                    rows[0],
                    rows[1],
                    row_sems.at[message, 0, side],
                    row_sems.at[message, 1, side],
                    (wrap(group - 1 + 2 * side, groups), tile),
                ),
            ]
        return copies

    at_east = (lane == LANES - 1) & (tile < tiles - 1)
    at_west = (lane == 0) & (tile > 0)
    at_north = (row == ROWS - 1) & (group < groups - 1)
    at_south = (row == 0) & (group > 0)

    def gathered(step, message, a, quad, u):
        k = quad * deep + u
        chunk, place_at = row_place(quad, u)
        east = pltpu.roll(lane_recv[message, 0, a], LANES - 1 - k, 1)
        west = pltpu.roll(lane_recv[message, 1, a], LANES - k, 1)
        north = row_recv[step, 0, chunk, a, pl.ds(place_at, 1), :]
        south = row_recv[step, 1, chunk, a, pl.ds(place_at, 1), :]
        return (
            partial[a, k]
            + jnp.where(at_east, east, 0.0)
            + jnp.where(at_west, west, 0.0)
            + jnp.where(at_north, jnp.broadcast_to(north, (ROWS, LANES)), 0.0)
            + jnp.where(at_south, jnp.broadcast_to(south, (ROWS, LANES)), 0.0)
        )

    relaxed = relax()

    def first_down(s, carry):
        landed(codes.at[s], code_sems.at[s])
        landed(scales.at[s], scale_sems.at[s])
        factors = [scales[s, pl.ds(a, 1), :] for a in range(2)]
        for u in range(share):
            k = s * share + u
            values = decode(codes[s, u])
            carry = downward(k, [values[a] * factors[a] for a in range(2)], relaxed, carry)
        return carry

    lax.fori_loop(0, tiles, first_down, (nothing, nothing))
    top = upward()
    surf_block[...] = next_surface(relaxed, top)

    def arrived_give(i, carry):
        quad = wrap(lax.div(tile, QUAD) - i, quads)
        for v in range(QUAD):
            s = quad * QUAD + v
            landed(currents.at[:, pl.ds(s * share, share)], current_sems.at[s])
        return give(0, quad, carry)

    edges = arrived_give(0, (nothing,) * 4)
    for n, (a, b) in enumerate(near):
        push(
            surf_block, around.at[n], send_sems.at[5], near_sems.at[2], near_device(a, b)
        ).start()
    edges = lax.fori_loop(1, quads, arrived_give, edges)
    keep_edges(0, edges)

    landed(around.at[pl.ds(0, len(near))], near_sems.at[2])
    for copy in edge_copies(0):
        copy.start()
    for a in range(2 * UP + 1):
        blocks = [surf_block if (a, b) == (UP, 1) else around.at[near.index((a, b))] for b in range(3)]
        place(FIELDS - 1, a, blocks[1][...], jnp.where(east_lanes, blocks[2][...], blocks[0][...]))
    relaxed_again = relax()
    for copy in edge_copies(0):
        copy.wait_recv()

    def second_down(quad, carry):
        for u in range(deep):
            sources = [gathered(0, 0, a, quad, u) for a in range(2)]
            carry = downward(quad * deep + u, sources, relaxed_again, carry)
        return carry

    lax.fori_loop(0, quads, second_down, (nothing, nothing))
    top = upward()
    surface_out[...] = next_surface(relaxed_again, top)

    turn = lax.div(lax.div(tile, QUAD), CHUNKS)

    def quad_of(chunk, i):
        return wrap(turn - i, quads // CHUNKS) * CHUNKS + chunk

    for chunk in range(CHUNKS):
        edges = lax.fori_loop(
            0,
            quads // CHUNKS,
            lambda i, carry, chunk=chunk: give(1, quad_of(chunk, i), carry),
            (nothing,) * 4,
        )
        keep_edges(1 + chunk, edges)
        for copy in edge_copies(1, chunk):
            copy.start()

    landed(currents.at[:, pl.ds(0, levels - share)], send_sems.at[0])
    landed(middle, send_sems.at[1])
    landed(sides, send_sems.at[2])
    landed(sent_codes.at[pl.ds(0, tiles - 1)], send_sems.at[3])
    landed(sent_scales.at[pl.ds(0, tiles - 1)], send_sems.at[4])
    landed(around.at[pl.ds(0, len(near))], send_sems.at[5])
    for copy in edge_copies(0):
        copy.wait_send()

    def back_refs(to):
        return [
            (back_codes.at[to], codes_out.at[:, :, lanes_of(tile)], 0),
            (back_scales.at[to], scales_out.at[:, lanes_of(tile)], 1),
        ]

    def send_back(quad):
        for v in range(QUAD):
            to = quad * QUAD + v

            @pl.when(to != tile)
            def _():
                for src, dst, n in back_refs(to):
                    push(src, dst, send_sems.at[6 + n], back_sems.at[n], (group, to)).start()

    for chunk in range(CHUNKS):
        for copy in edge_copies(1, chunk):
            copy.wait_recv()

        def finish(i, _, chunk=chunk):
            quad = quad_of(chunk, i)
            for v in range(QUAD):
                values = [
                    [gathered(1, 1 + chunk, a, quad, v * share + u) for u in range(share)]
                    for a in range(2)
                ]
                encode(values, quad * QUAD + v, back_codes, back_scales)

            @pl.when(i > 0)
            def _():
                send_back(quad_of(chunk, i - 1))

            return 0

        lax.fori_loop(0, quads // CHUNKS, finish, 0)
        send_back(quad_of(chunk, quads // CHUNKS - 1))
    for src, dst, n in back_refs(tile):
        pltpu.make_async_copy(src, dst, back_sems.at[n]).start()

    for chunk in range(CHUNKS):
        for copy in edge_copies(1, chunk):
            copy.wait_send()
    landed(back_codes.at[pl.ds(0, tiles - 1)], send_sems.at[6])
    landed(back_scales.at[pl.ds(0, tiles - 1)], send_sems.at[7])
    landed(codes_out, back_sems.at[0])
    landed(scales_out, back_sems.at[1])


def unpack(codes, scales, surface, tracer_out, surface_out):
    for u in range(codes.shape[0]):
        values = decode(codes[u])
        for a in range(2):
            tracer_out[a, u] = values[a] * scales[pl.ds(a, 1), :]
    surface_out[...] = surface[...]


def local(
    tracer_adjoint,
    surface_adjoint,
    velocity,
    vertical_coupling,
    ocean_levels,
    face_conductance,
    buoyancy_weights,
    surface_flux,
):
    groups, tiles = lax.axis_size("grp"), lax.axis_size("tile")
    levels = vertical_coupling.shape[0]
    share = levels // tiles
    cells = (ROWS, LANES)
    blocks = 2 * UP + 1
    f32, i32 = jnp.float32, jnp.int32
    anywhere = pl.BlockSpec(memory_space=pl.ANY)
    vmem = pl.BlockSpec(memory_space=pltpu.VMEM)
    dma = pltpu.SemaphoreType.DMA
    packed = (tiles, share) + cells
    codes, scales, surface = pl.pallas_call(
        functools.partial(kernel, (groups, tiles, share, levels)),
        out_shape=(
            jax.ShapeDtypeStruct((share, ROWS, tiles * LANES), i32),
            jax.ShapeDtypeStruct((2, tiles * LANES), f32),
            jax.ShapeDtypeStruct(surface_adjoint.shape, f32),
        ),
        in_specs=[anywhere] * 8,
        out_specs=(anywhere, anywhere, vmem),
        scratch_shapes=[
            pltpu.VMEM(tracer_adjoint.shape, f32),
            pltpu.VMEM(cells, f32),
            pltpu.VMEM(vertical_coupling.shape, f32),
            pltpu.VMEM(cells, i32),
            pltpu.VMEM((4,) + cells, f32),
            pltpu.SMEM(buoyancy_weights.shape, f32),
            pltpu.SMEM(surface_flux.shape, f32),
            pltpu.VMEM(packed, i32),
            pltpu.VMEM((tiles, 2, LANES), f32),
            pltpu.VMEM(packed, i32),
            pltpu.VMEM((tiles, 2, LANES), f32),
            pltpu.VMEM((2, levels) + cells, jnp.bfloat16),
            pltpu.VMEM(packed, i32),
            pltpu.VMEM((tiles, 2, LANES), f32),
            pltpu.VMEM((FIELDS,) + cells, f32),
            pltpu.VMEM(cells, f32),
            pltpu.VMEM((blocks - 1, FIELDS) + cells, f32),
            pltpu.VMEM((blocks, 2) + cells, f32),
            pltpu.VMEM((3 * blocks - 1,) + cells, f32),
            pltpu.VMEM((FIELDS, HIGH, 2 * LANES), f32),
            pltpu.VMEM((4, HIGH, 2 * LANES), f32),
            pltpu.VMEM((levels,) + cells, f32),
            pltpu.VMEM((levels,) + cells, f32),
            pltpu.VMEM((levels,) + cells, f32),
            pltpu.VMEM((2, levels) + cells, f32),
            pltpu.VMEM((2, levels) + cells, f32),
            pltpu.VMEM(cells, f32),
            pltpu.VMEM((1 + CHUNKS, 2, 2) + cells, f32),
            pltpu.VMEM((1 + CHUNKS, 2, 2) + cells, f32),
            pltpu.VMEM((STEPS, 2, CHUNKS, 2, levels // CHUNKS, LANES), f32),
            pltpu.VMEM((STEPS, 2, CHUNKS, 2, levels // CHUNKS, LANES), f32),
            dma((7,)),
            dma((tiles,)),
            dma((tiles,)),
            dma((tiles,)),
            dma((8,)),
            dma((2,)),
            dma((3,)),
            dma((1 + CHUNKS, 2, 2)),
            dma((1 + CHUNKS, 2, 2)),
        ],
        compiler_params=pltpu.CompilerParams(collective_id=0, has_side_effects=True),
    )(
        tracer_adjoint,
        surface_adjoint,
        velocity,
        vertical_coupling,
        ocean_levels,
        face_conductance,
        buoyancy_weights,
        surface_flux,
    )
    return pl.pallas_call(
        unpack,
        out_shape=(
            jax.ShapeDtypeStruct(tracer_adjoint.shape, f32),
            jax.ShapeDtypeStruct(surface_adjoint.shape, f32),
        ),
        in_specs=[vmem] * 3,
        out_specs=(vmem, vmem),
    )(codes, scales, surface)


def solution(mesh):
    in_specs = (
        P(None, "tile", "grp", None),
        P("grp", "tile"),
        P(None, "tile", "grp", None),
        P(None, "grp", "tile"),
        P("grp", "tile"),
        P(None, "grp", "tile"),
        P(),
        P(),
    )
    out_specs = (P(None, "tile", "grp", None), P("grp", "tile"))
    return jax.shard_map(local, mesh=mesh, in_specs=in_specs, out_specs=out_specs, check_vma=False)
```

time: 77.6 us -> 66.8 us (0.86)
  the two profiles are of different devices: /device:TPU:1 before, /device:TPU:8 now
where the time goes in v2:
time: 66.8 us; the launch traced here: 66.7 us
  Pallas kernels  66 us (99%)
    pallas_call x1, Pallas kernels, local(): pl.pallas_call(functools.partial(kernel, (groups, tiles, share, levels)),...  64 us
    pallas_call x1, Pallas kernels, local(): pl.pallas_call(unpack, out_shape=(jax.ShapeDtypeStruct(tracer_adjoint.sha...  2.01 us

profile of v2, /device:TPU:8, one launch (start us, length us, event | category | flops | bytes accessed | tf_op | source)
XLA Modules:
  0.0 66.7 jit_solution(9484797560150381086)
XLA Ops:
  0.6 64.0 %shard_map.95 = (s32[3,8,4096]{2,1,0:T(8,128)}, f32[2,4096]{1,0:T(2,128)}, f32[8,128]{1,0:T(8,128)}) custom-call(f32[2,3,8,4096]{3,2,1,0:T(8,128)} %tracer_in.1, f32[8,128]{1,0:T(8,128)} %surface_in.1, bf16[2,3,8,4096]{3,2,1,0:T(8,128)(2,1)} %velocity.1, f32[96,8,128]{2,1,0:T(8,128)} %coupling_in.1, s32[8,128]{1,0:T(8,128)} %ocean_levels.1, ...), custom_call_target="tpu_custom_call" | custom-call | tf_op jit(solution)/shard_map/pallas_call | solution.py:574
  64.7 2.0 %shard_map.96 = (f32[2,3,8,4096]{3,2,1,0:T(8,128)}, f32[8,128]{1,0:T(8,128)}) custom-call(s32[3,8,4096]{2,1,0:T(8,128)} %get-tuple-element.5.codes, f32[2,4096]{1,0:T(2,128)} %get-tuple-element.6.scales, f32[8,128]{1,0:T(8,128)} %get-tuple-element.7.surface), custom_call_target="tpu_custom_call" | custom-call | tf_op jit(solution)/shard_map/pallas_call | solution.py:636

commit v3 on v2

--- a/solution.py
+++ b/solution.py
@@ -111,12 +111,18 @@
     deep = QUAD * share
     group = lax.axis_index("grp")
     tile = lax.axis_index("tile")
-    near = [
-        (a, b) for a in range(2 * UP + 1) for b in range(3) if (a, b) != (UP, 1)
-    ]
-
     def near_device(a, b):
-        return (wrap(group - (a - UP), groups), wrap(tile - (b - 1), tiles))
+        return (group - (a - UP), wrap(tile - (b - 1), tiles))
+
+    above = [(group + a >= 0) & (group + a < groups) for a in range(-UP, UP + 1)]
+    below = above[::-1]
+
+    def where_present(present, action):
+        for a in range(2 * UP + 1):
+            if a == UP:
+                action(a)
+            else:
+                pl.when(present[a])(functools.partial(action, a))
 
     loads = [
         pltpu.make_async_copy(src, dst, load_sems.at[n])
@@ -143,14 +149,22 @@
         return 0
 
     lax.fori_loop(1, tiles, greet, 0)
-    greeted = tiles - 1
-    for a, b in near:
-        if a != UP:
-            greeted += 1
-            pl.semaphore_signal(barrier, inc=1, device_id=near_device(a, b), device_id_type=MESH)
+
+    def greet_rows(a):
+        for b in range(3):
+            if a != UP:
+                pl.semaphore_signal(
+                    barrier, inc=1, device_id=near_device(a, b), device_id_type=MESH
+                )
+
+    where_present(below, greet_rows)
     for load in loads[1:]:
         load.start()
-    pl.semaphore_wait(barrier, greeted)
+
+    rows_near = 0
+    for a in range(1, UP + 1):
+        rows_near += (group + groups - a) // groups + (2 * groups - 1 - group - a) // groups
+    pl.semaphore_wait(barrier, tiles - 1 + 3 * rows_near)
 
     def others(action, first=1, last=tiles):
         def one(i, _):
@@ -219,26 +233,53 @@
     def middle_slot(a):
         return a if a < UP else a - 1
 
-    for a, b in near:
-        if b == 1:
-            push(
-                mine,
-                middle.at[middle_slot(a)],
-                send_sems.at[1],
-                near_sems.at[0],
-                near_device(a, b),
-            ).start()
-        else:
-            push(
-                mine_edge, sides.at[a, b // 2], send_sems.at[2], near_sems.at[1], near_device(a, b)
-            ).start()
+    def send_fields(a):
+        for b in range(3):
+            if b != 1:
+                push(
+                    mine_edge,
+                    sides.at[a, b // 2],
+                    near_sems.at[1, 0, a],
+                    near_sems.at[1, 1, a],
+                    near_device(a, b),
+                ).start()
+            elif a != UP:
+                push(
+                    mine,
+                    middle.at[middle_slot(a)],
+                    near_sems.at[0, 0, a],
+                    near_sems.at[0, 1, a],
+                    near_device(a, b),
+                ).start()
+
+    def fields_passed(a, way):
+        landed(sides.at[a], near_sems.at[1, way, a])
+        if a != UP:
+            landed(middle.at[middle_slot(a)], near_sems.at[0, way, a])
+
+    def send_around(a):
+        for b in range(3):
+            if (a, b) != (UP, 1):
+                push(
+                    surf_block,
+                    around.at[a, b],
+                    near_sems.at[2, 0, a],
+                    near_sems.at[2, 1, a],
+                    near_device(a, b),
+                ).start()
+
+    def around_passed(a, way):
+        blocks = around.at[a, pl.ds(0, 2)] if a == UP else around.at[a]
+        landed(blocks, near_sems.at[2, way, a])
+
+    where_present(below, send_fields)
 
     def send_codes(to):
         push(
-            sent_codes.at[to], codes.at[tile], send_sems.at[3], code_sems.at[tile], (group, to)
+            sent_codes.at[to], codes.at[tile], send_sems.at[1], code_sems.at[tile], (group, to)
         ).start()
         push(
-            sent_scales.at[to], scales.at[tile], send_sems.at[4], scale_sems.at[tile], (group, to)
+            sent_scales.at[to], scales.at[tile], send_sems.at[2], scale_sems.at[tile], (group, to)
         ).start()
 
     others(send_codes)
@@ -263,21 +304,17 @@
     nothing = jnp.zeros((ROWS, LANES), jnp.float32)
     lax.fori_loop(0, levels, factor, (nothing, nothing))
 
-    row_inside = [
-        (group + (a - UP) >= 0) & (group + (a - UP) < groups) for a in range(2 * UP + 1)
-    ]
     east_lanes = lane < EDGE
     side_inside = (east_lanes & (tile < tiles - 1)) | ((lane >= LANES - EDGE) & (tile > 0))
 
     def place(f, a, middle_block, side_block):
         rows = pl.ds(a * ROWS, ROWS)
-        fields[f, rows, pl.ds(0, LANES)] = jnp.where(row_inside[a], middle_block, 0.0)
+        fields[f, rows, pl.ds(0, LANES)] = jnp.where(above[a], middle_block, 0.0)
         fields[f, rows, pl.ds(LANES, LANES)] = jnp.where(
-            side_inside & row_inside[a], side_block, 0.0
+            side_inside & above[a], side_block, 0.0
         )
 
-    landed(middle, near_sems.at[0])
-    landed(sides, near_sems.at[1])
+    where_present(above, lambda a: fields_passed(a, 1))
     for a in range(2 * UP + 1):
         from_west, from_east = sides[a, 0], sides[a, 1]
         for f in range(FIELDS):
@@ -374,27 +411,34 @@
             for side in range(2):
                 lane_send[message, side, a] = edges[2 * a + side]
 
-    def edge_copies(step, chunk=None):
+    def edge_copies(way, step, chunk=None):
         message = 0 if chunk is None else 1 + chunk
         copies = []
         for side in range(2):
             rows = [ref.at[step, side] for ref in (row_send, row_recv)]
             if chunk is not None:
                 rows = [ref.at[chunk] for ref in rows]
+            southern, northern = group > 0, group < groups - 1
             copies += [
-                push(
-                    lane_send.at[message, side],
-                    lane_recv.at[message, side],
-                    lane_sems.at[message, 0, side],
-                    lane_sems.at[message, 1, side],
-                    (group, wrap(tile - 1 + 2 * side, tiles)),
+                (
+                    (southern, northern)[side if way == 0 else 1 - side],
+                    push(
+                        rows[0],
+                        rows[1],
+                        row_sems.at[message, 0, side],
+                        row_sems.at[message, 1, side],
+                        (group - 1 + 2 * side, tile),
+                    ),
                 ),
-                push(
-                    rows[0],
-                    rows[1],
-                    row_sems.at[message, 0, side],
-                    row_sems.at[message, 1, side],
-                    (wrap(group - 1 + 2 * side, groups), tile),
+                (
+                    group >= 0,
+                    push(
+                        lane_send.at[message, side],
+                        lane_recv.at[message, side],
+                        lane_sems.at[message, 0, side],
+                        lane_sems.at[message, 1, side],
+                        (group, wrap(tile - 1 + 2 * side, tiles)),
+                    ),
                 ),
             ]
         return copies
@@ -443,22 +487,19 @@
         return give(0, quad, carry)
 
     edges = arrived_give(0, (nothing,) * 4)
-    for n, (a, b) in enumerate(near):
-        push(
-            surf_block, around.at[n], send_sems.at[5], near_sems.at[2], near_device(a, b)
-        ).start()
+    where_present(below, send_around)
     edges = lax.fori_loop(1, quads, arrived_give, edges)
     keep_edges(0, edges)
 
-    landed(around.at[pl.ds(0, len(near))], near_sems.at[2])
-    for copy in edge_copies(0):
-        copy.start()
+    for present, copy in edge_copies(0, 0):
+        pl.when(present)(copy.start)
+    where_present(above, lambda a: around_passed(a, 1))
     for a in range(2 * UP + 1):
-        blocks = [surf_block if (a, b) == (UP, 1) else around.at[near.index((a, b))] for b in range(3)]
+        blocks = [surf_block if (a, b) == (UP, 1) else around.at[a, b] for b in range(3)]
         place(FIELDS - 1, a, blocks[1][...], jnp.where(east_lanes, blocks[2][...], blocks[0][...]))
     relaxed_again = relax()
-    for copy in edge_copies(0):
-        copy.wait_recv()
+    for present, copy in edge_copies(1, 0):
+        pl.when(present)(copy.wait_recv)
 
     def second_down(quad, carry):
         for u in range(deep):
@@ -483,17 +524,20 @@
             (nothing,) * 4,
         )
         keep_edges(1 + chunk, edges)
-        for copy in edge_copies(1, chunk):
-            copy.start()
+        for present, copy in edge_copies(0, 1, chunk):
+            pl.when(present)(copy.start)
 
     landed(currents.at[:, pl.ds(0, levels - share)], send_sems.at[0])
-    landed(middle, send_sems.at[1])
-    landed(sides, send_sems.at[2])
-    landed(sent_codes.at[pl.ds(0, tiles - 1)], send_sems.at[3])
-    landed(sent_scales.at[pl.ds(0, tiles - 1)], send_sems.at[4])
-    landed(around.at[pl.ds(0, len(near))], send_sems.at[5])
-    for copy in edge_copies(0):
-        copy.wait_send()
+    landed(sent_codes.at[pl.ds(0, tiles - 1)], send_sems.at[1])
+    landed(sent_scales.at[pl.ds(0, tiles - 1)], send_sems.at[2])
+
+    def near_sent(a):
+        fields_passed(a, 0)
+        around_passed(a, 0)
+
+    where_present(below, near_sent)
+    for present, copy in edge_copies(0, 0):
+        pl.when(present)(copy.wait_send)
 
     def back_refs(to):
         return [
@@ -508,11 +552,11 @@
             @pl.when(to != tile)
             def _():
                 for src, dst, n in back_refs(to):
-                    push(src, dst, send_sems.at[6 + n], back_sems.at[n], (group, to)).start()
+                    push(src, dst, send_sems.at[3 + n], back_sems.at[n], (group, to)).start()
 
     for chunk in range(CHUNKS):
-        for copy in edge_copies(1, chunk):
-            copy.wait_recv()
+        for present, copy in edge_copies(1, 1, chunk):
+            pl.when(present)(copy.wait_recv)
 
         def finish(i, _, chunk=chunk):
             quad = quad_of(chunk, i)
@@ -535,10 +579,10 @@
         pltpu.make_async_copy(src, dst, back_sems.at[n]).start()
 
     for chunk in range(CHUNKS):
-        for copy in edge_copies(1, chunk):
-            copy.wait_send()
-    landed(back_codes.at[pl.ds(0, tiles - 1)], send_sems.at[6])
-    landed(back_scales.at[pl.ds(0, tiles - 1)], send_sems.at[7])
+        for present, copy in edge_copies(0, 1, chunk):
+            pl.when(present)(copy.wait_send)
+    landed(back_codes.at[pl.ds(0, tiles - 1)], send_sems.at[3])
+    landed(back_scales.at[pl.ds(0, tiles - 1)], send_sems.at[4])
     landed(codes_out, back_sems.at[0])
     landed(scales_out, back_sems.at[1])
 
@@ -599,7 +643,7 @@
             pltpu.VMEM(cells, f32),
             pltpu.VMEM((blocks - 1, FIELDS) + cells, f32),
             pltpu.VMEM((blocks, 2) + cells, f32),
-            pltpu.VMEM((3 * blocks - 1,) + cells, f32),
+            pltpu.VMEM((blocks, 3) + cells, f32),
             pltpu.VMEM((FIELDS, HIGH, 2 * LANES), f32),
             pltpu.VMEM((4, HIGH, 2 * LANES), f32),
             pltpu.VMEM((levels,) + cells, f32),
@@ -616,9 +660,9 @@
             dma((tiles,)),
             dma((tiles,)),
             dma((tiles,)),
-            dma((8,)),
+            dma((5,)),
             dma((2,)),
-            dma((3,)),
+            dma((3, 2, blocks)),
             dma((1 + CHUNKS, 2, 2)),
             dma((1 + CHUNKS, 2, 2)),
         ],

time: 66.8 us -> 60.6 us (0.907)
  the two profiles are of different devices: /device:TPU:8 before, /device:TPU:143 now
where the time goes in v3:
time: 60.6 us; the launch traced here: 60.4 us
  Pallas kernels  59.8 us (99%)
  between operations  0.64 us (1%)
    pallas_call x1, Pallas kernels, local(): pl.pallas_call(functools.partial(kernel, (groups, tiles, share, levels)),...  57.8 us
    pallas_call x1, Pallas kernels, local(): pl.pallas_call(unpack, out_shape=(jax.ShapeDtypeStruct(tracer_adjoint.sha...  2.01 us

profile of v3, /device:TPU:143, one launch (start us, length us, event | category | flops | bytes accessed | tf_op | source)
XLA Modules:
  0.0 60.4 jit_solution(2696467045065888012)
XLA Ops:
  0.6 57.8 %shard_map.95 = (s32[3,8,4096]{2,1,0:T(8,128)}, f32[2,4096]{1,0:T(2,128)}, f32[8,128]{1,0:T(8,128)}) custom-call(f32[2,3,8,4096]{3,2,1,0:T(8,128)} %tracer_in.1, f32[8,128]{1,0:T(8,128)} %surface_in.1, bf16[2,3,8,4096]{3,2,1,0:T(8,128)(2,1)} %velocity.1, f32[96,8,128]{2,1,0:T(8,128)} %coupling_in.1, s32[8,128]{1,0:T(8,128)} %ocean_levels.1, ...), custom_call_target="tpu_custom_call" | custom-call | tf_op jit(solution)/shard_map/pallas_call | solution.py:618
  58.4 2.0 %shard_map.96 = (f32[2,3,8,4096]{3,2,1,0:T(8,128)}, f32[8,128]{1,0:T(8,128)}) custom-call(s32[3,8,4096]{2,1,0:T(8,128)} %get-tuple-element.5.codes, f32[2,4096]{1,0:T(2,128)} %get-tuple-element.6.scales, f32[8,128]{1,0:T(8,128)} %get-tuple-element.7.surface), custom_call_target="tpu_custom_call" | custom-call | tf_op jit(solution)/shard_map/pallas_call | solution.py:680

commit v4 on v3

--- a/solution.py
+++ b/solution.py
@@ -142,13 +142,10 @@
 
     barrier = pltpu.get_barrier_semaphore()
 
-    def greet(i, _):
+    for i in range(1, tiles):
         pl.semaphore_signal(
             barrier, inc=1, device_id=(group, wrap(tile + i, tiles)), device_id_type=MESH
         )
-        return 0
-
-    lax.fori_loop(1, tiles, greet, 0)
 
     def greet_rows(a):
         for b in range(3):
@@ -374,14 +371,28 @@
     def next_surface(relaxed, top):
         return relaxed + jnp.where(0 < depth, flux[0] * top[0] + flux[1] * top[1], 0.0)
 
-    def row_place(quad, u):
-        return (lax.rem(quad, CHUNKS), lax.div(quad, CHUNKS) * deep + u)
+    def row_place(quad):
+        return (lax.rem(quad, CHUNKS), lax.div(quad, CHUNKS))
+
+    southern, northern = group > 0, group < groups - 1
+
+    def send_rows(step, message, quad, ready=None):
+        chunk, half = row_place(quad)
+        for side, present in enumerate((southern, northern)):
+            copy = push(
+                row_send.at[step, side, chunk, half],
+                row_recv.at[step, side, chunk, half],
+                row_sems.at[message, 0, side],
+                row_sems.at[message, 1, side],
+                (group - 1 + 2 * side, tile),
+            )
+            pl.when(present if ready is None else present & ready)(copy.start)
 
     def give(step, quad, carry):
         carry = list(carry)
+        chunk, half = row_place(quad)
         for u in range(deep):
             k = quad * deep + u
-            chunk, place_at = row_place(quad, u)
             zonal = 0.5 * currents[0, k].astype(jnp.float32)
             meridional = 0.5 * currents[1, k].astype(jnp.float32)
             for a in range(2):
@@ -402,8 +413,9 @@
                 carry[2 * a + 1] = jnp.where(
                     at_level, pltpu.roll(eastward, k + 1, 1), carry[2 * a + 1]
                 )
-                row_send[step, 0, chunk, a, pl.ds(place_at, 1), :] = southward[0:1]
-                row_send[step, 1, chunk, a, pl.ds(place_at, 1), :] = northward[0:1]
+                at_row = pl.ds(a * deep + u, 1)
+                row_send[step, 0, chunk, half, at_row, :] = southward[0:1]
+                row_send[step, 1, chunk, half, at_row, :] = northward[0:1]
         return tuple(carry)
 
     def keep_edges(message, edges):
@@ -411,37 +423,27 @@
             for side in range(2):
                 lane_send[message, side, a] = edges[2 * a + side]
 
-    def edge_copies(way, step, chunk=None):
-        message = 0 if chunk is None else 1 + chunk
-        copies = []
+    def lane_copies(message):
+        return [
+            push(
+                lane_send.at[message, side],
+                lane_recv.at[message, side],
+                lane_sems.at[message, 0, side],
+                lane_sems.at[message, 1, side],
+                (group, wrap(tile - 1 + 2 * side, tiles)),
+            )
+            for side in range(2)
+        ]
+
+    def rows_passed(way, step, message):
         for side in range(2):
-            rows = [ref.at[step, side] for ref in (row_send, row_recv)]
-            if chunk is not None:
-                rows = [ref.at[chunk] for ref in rows]
-            southern, northern = group > 0, group < groups - 1
-            copies += [
-                (
-                    (southern, northern)[side if way == 0 else 1 - side],
-                    push(
-                        rows[0],
-                        rows[1],
-                        row_sems.at[message, 0, side],
-                        row_sems.at[message, 1, side],
-                        (group - 1 + 2 * side, tile),
-                    ),
-                ),
-                (
-                    group >= 0,
-                    push(
-                        lane_send.at[message, side],
-                        lane_recv.at[message, side],
-                        lane_sems.at[message, 0, side],
-                        lane_sems.at[message, 1, side],
-                        (group, wrap(tile - 1 + 2 * side, tiles)),
-                    ),
-                ),
-            ]
-        return copies
+            rows = row_recv.at[step, side]
+            if step:
+                rows = rows.at[message - 1]
+            present = (southern, northern)[side if way == 0 else 1 - side]
+            pl.when(present)(
+                functools.partial(landed, rows, row_sems.at[message, way, side])
+            )
 
     at_east = (lane == LANES - 1) & (tile < tiles - 1)
     at_west = (lane == 0) & (tile > 0)
@@ -450,11 +452,12 @@
 
     def gathered(step, message, a, quad, u):
         k = quad * deep + u
-        chunk, place_at = row_place(quad, u)
+        chunk, half = row_place(quad)
+        at_row = pl.ds(a * deep + u, 1)
         east = pltpu.roll(lane_recv[message, 0, a], LANES - 1 - k, 1)
         west = pltpu.roll(lane_recv[message, 1, a], LANES - k, 1)
-        north = row_recv[step, 0, chunk, a, pl.ds(place_at, 1), :]
-        south = row_recv[step, 1, chunk, a, pl.ds(place_at, 1), :]
+        north = row_recv[step, 0, chunk, half, at_row, :]
+        south = row_recv[step, 1, chunk, half, at_row, :]
         return (
             partial[a, k]
             + jnp.where(at_east, east, 0.0)
@@ -479,8 +482,11 @@
     top = upward()
     surf_block[...] = next_surface(relaxed, top)
 
+    def arrived_quad(i):
+        return wrap(lax.div(tile, QUAD) - i, quads)
+
     def arrived_give(i, carry):
-        quad = wrap(lax.div(tile, QUAD) - i, quads)
+        quad = arrived_quad(i)
         for v in range(QUAD):
             s = quad * QUAD + v
             landed(currents.at[:, pl.ds(s * share, share)], current_sems.at[s])
@@ -488,18 +494,25 @@
 
     edges = arrived_give(0, (nothing,) * 4)
     where_present(below, send_around)
-    edges = lax.fori_loop(1, quads, arrived_give, edges)
+
+    def send_and_give(i, carry):
+        send_rows(0, 0, arrived_quad(i - 1))
+        return arrived_give(i, carry)
+
+    edges = lax.fori_loop(1, quads, send_and_give, edges)
     keep_edges(0, edges)
-
-    for present, copy in edge_copies(0, 0):
-        pl.when(present)(copy.start)
+    send_rows(0, 0, arrived_quad(quads - 1))
+
+    for copy in lane_copies(0):
+        copy.start()
     where_present(above, lambda a: around_passed(a, 1))
     for a in range(2 * UP + 1):
         blocks = [surf_block if (a, b) == (UP, 1) else around.at[a, b] for b in range(3)]
         place(FIELDS - 1, a, blocks[1][...], jnp.where(east_lanes, blocks[2][...], blocks[0][...]))
     relaxed_again = relax()
-    for present, copy in edge_copies(1, 0):
-        pl.when(present)(copy.wait_recv)
+    for copy in lane_copies(0):
+        copy.wait_recv()
+    rows_passed(1, 0, 0)
 
     def second_down(quad, carry):
         for u in range(deep):
@@ -517,15 +530,16 @@
         return wrap(turn - i, quads // CHUNKS) * CHUNKS + chunk
 
     for chunk in range(CHUNKS):
-        edges = lax.fori_loop(
-            0,
-            quads // CHUNKS,
-            lambda i, carry, chunk=chunk: give(1, quad_of(chunk, i), carry),
-            (nothing,) * 4,
-        )
+
+        def give_and_send(i, carry, chunk=chunk):
+            send_rows(1, 1 + chunk, quad_of(chunk, i - 1), i > 0)
+            return give(1, quad_of(chunk, i), carry)
+
+        edges = lax.fori_loop(0, quads // CHUNKS, give_and_send, (nothing,) * 4)
         keep_edges(1 + chunk, edges)
-        for present, copy in edge_copies(0, 1, chunk):
-            pl.when(present)(copy.start)
+        send_rows(1, 1 + chunk, quad_of(chunk, quads // CHUNKS - 1))
+        for copy in lane_copies(1 + chunk):
+            copy.start()
 
     landed(currents.at[:, pl.ds(0, levels - share)], send_sems.at[0])
     landed(sent_codes.at[pl.ds(0, tiles - 1)], send_sems.at[1])
@@ -536,8 +550,9 @@
         around_passed(a, 0)
 
     where_present(below, near_sent)
-    for present, copy in edge_copies(0, 0):
-        pl.when(present)(copy.wait_send)
+    for copy in lane_copies(0):
+        copy.wait_send()
+    rows_passed(0, 0, 0)
 
     def back_refs(to):
         return [
@@ -555,8 +570,9 @@
                     push(src, dst, send_sems.at[3 + n], back_sems.at[n], (group, to)).start()
 
     for chunk in range(CHUNKS):
-        for present, copy in edge_copies(1, 1, chunk):
-            pl.when(present)(copy.wait_recv)
+        for copy in lane_copies(1 + chunk):
+            copy.wait_recv()
+        rows_passed(1, 1, 1 + chunk)
 
         def finish(i, _, chunk=chunk):
             quad = quad_of(chunk, i)
@@ -579,8 +595,9 @@
         pltpu.make_async_copy(src, dst, back_sems.at[n]).start()
 
     for chunk in range(CHUNKS):
-        for present, copy in edge_copies(0, 1, chunk):
-            pl.when(present)(copy.wait_send)
+        for copy in lane_copies(1 + chunk):
+            copy.wait_send()
+        rows_passed(0, 1, 1 + chunk)
     landed(back_codes.at[pl.ds(0, tiles - 1)], send_sems.at[3])
     landed(back_scales.at[pl.ds(0, tiles - 1)], send_sems.at[4])
     landed(codes_out, back_sems.at[0])
@@ -611,19 +628,20 @@
     cells = (ROWS, LANES)
     blocks = 2 * UP + 1
     f32, i32 = jnp.float32, jnp.int32
-    anywhere = pl.BlockSpec(memory_space=pl.ANY)
     vmem = pl.BlockSpec(memory_space=pltpu.VMEM)
     dma = pltpu.SemaphoreType.DMA
     packed = (tiles, share) + cells
+    quads = tiles // QUAD
+    row_blocks = (CHUNKS, quads // CHUNKS, 2 * QUAD * share, LANES)
     codes, scales, surface = pl.pallas_call(
         functools.partial(kernel, (groups, tiles, share, levels)),
         out_shape=(
-            jax.ShapeDtypeStruct((share, ROWS, tiles * LANES), i32),
-            jax.ShapeDtypeStruct((2, tiles * LANES), f32),
-            jax.ShapeDtypeStruct(surface_adjoint.shape, f32),
+            pltpu.VMEM((share, ROWS, tiles * LANES), i32),
+            pltpu.VMEM((2, tiles * LANES), f32),
+            pltpu.VMEM(surface_adjoint.shape, f32),
         ),
-        in_specs=[anywhere] * 8,
-        out_specs=(anywhere, anywhere, vmem),
+        in_specs=[pl.BlockSpec(memory_space=pltpu.HBM)] * 8,
+        out_specs=(vmem,) * 3,
         scratch_shapes=[
             pltpu.VMEM(tracer_adjoint.shape, f32),
             pltpu.VMEM(cells, f32),
@@ -654,8 +672,8 @@
             pltpu.VMEM(cells, f32),
             pltpu.VMEM((1 + CHUNKS, 2, 2) + cells, f32),
             pltpu.VMEM((1 + CHUNKS, 2, 2) + cells, f32),
-            pltpu.VMEM((STEPS, 2, CHUNKS, 2, levels // CHUNKS, LANES), f32),
-            pltpu.VMEM((STEPS, 2, CHUNKS, 2, levels // CHUNKS, LANES), f32),
+            pltpu.VMEM((STEPS, 2) + row_blocks, f32),
+            pltpu.VMEM((STEPS, 2) + row_blocks, f32),
             dma((7,)),
             dma((tiles,)),
             dma((tiles,)),
@@ -666,16 +684,23 @@
             dma((1 + CHUNKS, 2, 2)),
             dma((1 + CHUNKS, 2, 2)),
         ],
-        compiler_params=pltpu.CompilerParams(collective_id=0, has_side_effects=True),
+        compiler_params=pltpu.CompilerParams(
+            collective_id=0, has_side_effects=True, vmem_limit_bytes=24 << 20
+        ),
     )(
-        tracer_adjoint,
-        surface_adjoint,
-        velocity,
-        vertical_coupling,
-        ocean_levels,
-        face_conductance,
-        buoyancy_weights,
-        surface_flux,
+        *[
+            pltpu.with_memory_space_constraint(value, pltpu.HBM)
+            for value in (
+                tracer_adjoint,
+                surface_adjoint,
+                velocity,
+                vertical_coupling,
+                ocean_levels,
+                face_conductance,
+                buoyancy_weights,
+                surface_flux,
+            )
+        ]
     )
     return pl.pallas_call(
         unpack,
@@ -685,6 +710,7 @@
         ),
         in_specs=[vmem] * 3,
         out_specs=(vmem, vmem),
+        compiler_params=pltpu.CompilerParams(vmem_limit_bytes=8 << 20),
     )(codes, scales, surface)
 
 

time: 60.6 us -> 58.6 us (0.967)
  the two profiles are of different devices: /device:TPU:143 before, /device:TPU:136 now
where the time goes in v4:
time: 58.6 us; the launch traced here: 58.5 us
  Pallas kernels  57.8 us (99%)
  between operations  0.64 us (1%)
    pallas_call x1, Pallas kernels, local(): pl.pallas_call(functools.partial(kernel, (groups, tiles, share, levels)),...  56.9 us

profile of v4, /device:TPU:136, one launch (start us, length us, event | category | flops | bytes accessed | tf_op | source)
XLA Modules:
  0.0 58.5 jit_solution(11542506804651297994)
XLA Ops:
  0.6 56.9 %shard_map.95 = (s32[3,8,4096]{2,1,0:T(8,128)S(1)}, f32[2,4096]{1,0:T(2,128)S(1)}, f32[8,128]{1,0:T(8,128)S(1)}) custom-call(f32[2,3,8,4096]{3,2,1,0:T(8,128)} %tracer_in.1, f32[8,128]{1,0:T(8,128)} %surface_in.1, bf16[2,3,8,4096]{3,2,1,0:T(8,128)(2,1)} %velocity.1, f32[96,8,128]{2,1,0:T(8,128)} %coupling_in.1, s32[8,128]{1,0:T(8,128)} %ocean_levels.1, ...), custom_call_target="tpu_custom_call" | custom-call | tf_op jit(solution)/shard_map/pallas_call | solution.py:636
  57.5 1.0 %shard_map.96 = (f32[2,3,8,4096]{3,2,1,0:T(8,128)}, f32[8,128]{1,0:T(8,128)}) custom-call(s32[3,8,4096]{2,1,0:T(8,128)S(1)} %get-tuple-element.5.codes, f32[2,4096]{1,0:T(2,128)S(1)} %get-tuple-element.6.scales, f32[8,128]{1,0:T(8,128)S(1)} %get-tuple-element.7.surface), custom_call_target="tpu_custom_call" | custom-call | tf_op jit(solution)/shard_map/pallas_call | solution.py:705

commit v5 on v4

--- a/solution.py
+++ b/solution.py
@@ -19,7 +19,7 @@
 EDGE = 16
 FIELDS = 4
 QUAD = 4
-CHUNKS = 2
+CHUNKS = 4
 EARLY = 8
 
 
@@ -56,7 +56,7 @@
     sizes,
     tracer_in,
     surface_in,
-    velocity,
+    velocity_in,
     coupling_in,
     ocean_levels,
     conductance_in,
@@ -66,6 +66,7 @@
     scales_out,
     surface_out,
     tracer,
+    velocity,
     surface,
     coupling,
     depths,
@@ -135,9 +136,11 @@
                 (coupling_in, coupling),
                 (weights_in, weights),
                 (flux_in, flux),
+                (velocity_in, velocity),
             ]
         )
     ]
+    loads[7].start()
     loads[0].start()
 
     barrier = pltpu.get_barrier_semaphore()
@@ -155,8 +158,9 @@
                 )
 
     where_present(below, greet_rows)
-    for load in loads[1:]:
+    for load in loads[1:7]:
         load.start()
+    loads[7].wait()
 
     rows_near = 0
     for a in range(1, UP + 1):
@@ -283,7 +287,7 @@
     pltpu.make_async_copy(sent_codes.at[tile], codes.at[tile], code_sems.at[tile]).start()
     pltpu.make_async_copy(sent_scales.at[tile], scales.at[tile], scale_sems.at[tile]).start()
     others(send_current, 1 + EARLY, tiles)
-    for load in loads[3:]:
+    for load in loads[3:7]:
         load.wait()
     depth = depths[...]
 
@@ -644,6 +648,7 @@
         out_specs=(vmem,) * 3,
         scratch_shapes=[
             pltpu.VMEM(tracer_adjoint.shape, f32),
+            pltpu.VMEM(velocity.shape, velocity.dtype),
             pltpu.VMEM(cells, f32),
             pltpu.VMEM(vertical_coupling.shape, f32),
             pltpu.VMEM(cells, i32),
@@ -674,7 +679,7 @@
             pltpu.VMEM((1 + CHUNKS, 2, 2) + cells, f32),
             pltpu.VMEM((STEPS, 2) + row_blocks, f32),
             pltpu.VMEM((STEPS, 2) + row_blocks, f32),
-            dma((7,)),
+            dma((8,)),
             dma((tiles,)),
             dma((tiles,)),
             dma((tiles,)),

time: 58.6 us -> 58.2 us (level)
  the two profiles are of different devices: /device:TPU:136 before, /device:TPU:248 now
where the time goes in v5:
time: 58.2 us; the launch traced here: 58.1 us
  Pallas kernels  57.4 us (99%)
  between operations  0.64 us (1%)
    pallas_call x1, Pallas kernels, local(): pl.pallas_call(functools.partial(kernel, (groups, tiles, share, levels)),...  56.4 us

profile of v5, /device:TPU:248, one launch (start us, length us, event | category | flops | bytes accessed | tf_op | source)
XLA Modules:
  0.0 58.1 jit_solution(4214263181519770490)
XLA Ops:
  0.6 56.4 %shard_map.95 = (s32[3,8,4096]{2,1,0:T(8,128)S(1)}, f32[2,4096]{1,0:T(2,128)S(1)}, f32[8,128]{1,0:T(8,128)S(1)}) custom-call(f32[2,3,8,4096]{3,2,1,0:T(8,128)} %tracer_in.1, f32[8,128]{1,0:T(8,128)} %surface_in.1, bf16[2,3,8,4096]{3,2,1,0:T(8,128)(2,1)} %velocity_in.1, f32[96,8,128]{2,1,0:T(8,128)} %coupling_in.1, s32[8,128]{1,0:T(8,128)} %ocean_levels.1, ...), custom_call_target="tpu_custom_call" | custom-call | tf_op jit(solution)/shard_map/pallas_call | solution.py:640
  57.1 1.0 %shard_map.96 = (f32[2,3,8,4096]{3,2,1,0:T(8,128)}, f32[8,128]{1,0:T(8,128)}) custom-call(s32[3,8,4096]{2,1,0:T(8,128)S(1)} %get-tuple-element.5.codes, f32[2,4096]{1,0:T(2,128)S(1)} %get-tuple-element.6.scales, f32[8,128]{1,0:T(8,128)S(1)} %get-tuple-element.7.surface), custom_call_target="tpu_custom_call" | custom-call | tf_op jit(solution)/shard_map/pallas_call | solution.py:710
